TPU v7x, 128 devices: a whole 4x4x4 slice. The times are simulated.
128 devices in a mesh: grp: 2 (over core), row: 16 (over y, x), col: 4 (over z).
Axes of the slice: x: 4, y: 4, z: 4, core: 2. Of those that a mesh axis runs over, the one named last changes fastest.
Arguments:
- root_inverse: bfloat16 [12288, 12288], P(('grp', 'row'), 'col'), may hold values from -0.0546875 to 0.0546875
- child_inverse: bfloat16 [2, 8192, 8192], P('grp', 'row', 'col'), may hold values from -0.0625 to 0.0625
- coupling: bfloat16 [2, 1536, 8192], P('grp', 'col', 'row'), may hold values from -0.0625 to 0.0625
- child_weights: bfloat16 [2, 8192], P('grp', 'col'), may hold values from 0.5 to 2
- root_weights: bfloat16 [12288], P('col'), may hold values from 0.5 to 2
- parent_blocks: int32 [2, 12], replicated, may hold values from 0 to 95, as said below
Outputs:
- grad_root: bfloat16 [12288, 12288], P(('grp', 'row'), 'col')
- grad_child: bfloat16 [2, 8192, 8192], P('grp', 'row', 'col')
- grad_coupling: bfloat16 [2, 1536, 8192], P('grp', 'col', 'row')
Inputs may be any that keep to these rules, and one draw needn't show every extreme that they name: `parent_blocks`: within one child the 12 blocks are distinct; child 0 always names block 0 and block 12288 // 128 - 1; the two children may share blocks.
All inputs are finite; a program needn't handle non-finite values.
Results may differ from a plain program's by a relative error of at most 0.0059.
Values may be sent and summed in bfloat16 or wider, within the bound.
A program may use at most 128 MiB of HBM per device.

v0:
```python
import jax
import jax.numpy as jnp
from jax import lax
from jax.sharding import PartitionSpec as P

BW = 128


def local(root_inverse, child_inverse, coupling, child_weights, root_weights, parent_blocks):
    col_index = lax.axis_index("col")
    col_count = lax.axis_size("col")
    root_rows, root_cols = root_inverse.shape
    local_blocks = root_cols // BW
    share_cols = coupling.shape[1]
    width = share_cols * col_count
    block_count = width // BW
    highest = lax.Precision.HIGHEST
    offset = parent_blocks - col_index * local_blocks
    block_ids = jnp.arange(local_blocks, dtype=jnp.int32)
    owners = [
        (offset[child][:, None] == block_ids[None, :]).astype(jnp.float32) for child in range(2)
    ]
    root_blocks = root_inverse.astype(jnp.float32).reshape(root_rows, local_blocks, BW)
    picks = []
    for child in range(2):
        taken = jnp.einsum("rkb,jk->rjb", root_blocks, owners[child], precision=highest)
        picks.append(taken.reshape(root_rows, width))
    picked = jnp.stack(picks, axis=1)
    selected = lax.psum(picked.astype(jnp.bfloat16), "col")
    mine = lax.dynamic_slice_in_dim(selected, col_index * share_cols, share_cols, 2)
    margin_part = jnp.concatenate(
        [
            jnp.dot(selected[:, child, :].T, mine[:, child, :], preferred_element_type=jnp.float32)
            for child in range(2)
        ],
        axis=0,
    )
    margin = lax.psum_scatter(margin_part, ("grp", "row"), scatter_dimension=0, tiled=True).astype(
        jnp.bfloat16
    )
    factor = child_inverse[0]
    links = coupling[0]
    weights = child_weights[0].astype(jnp.float32)
    links_all = lax.all_gather(links, "col", axis=0, tiled=True)
    solved = lax.psum_scatter(
        jnp.dot(links_all, factor, preferred_element_type=jnp.float32),
        "row",
        scatter_dimension=0,
        tiled=True,
    ).astype(jnp.bfloat16)
    solved_all = lax.all_gather(solved, "row", axis=0, tiled=True)
    scaled = (solved.astype(jnp.float32) * weights[None, :]).astype(jnp.bfloat16)
    adjoint_t = lax.psum_scatter(
        jnp.dot(solved_all, scaled.T, preferred_element_type=jnp.float32),
        "col",
        scatter_dimension=0,
        tiled=True,
    ).astype(jnp.bfloat16)
    adjoint_cols = lax.all_gather(adjoint_t, ("grp", "row"), axis=1, tiled=True).reshape(
        share_cols, 2, width
    )
    lifted = jnp.stack(
        [
            jnp.dot(
                selected[:, child, :],
                adjoint_cols[:, child, :].T,
                preferred_element_type=jnp.float32,
            )
            for child in range(2)
        ],
        axis=1,
    ).astype(jnp.bfloat16)
    lifted_all = lax.all_gather(lifted, "col", axis=2, tiled=True).reshape(
        root_rows, 2, block_count, BW
    )
    placed = jnp.zeros((root_rows, local_blocks, BW), jnp.float32)
    for child in range(2):
        spread = lifted_all[:, child].astype(jnp.float32)
        placed = placed + jnp.einsum("rjb,jk->rkb", spread, owners[child], precision=highest)
    placed = placed.reshape(root_rows, root_cols)
    root_scale = root_weights.astype(jnp.float32)[None, :]
    grad_root = (2.0 * root_inverse.astype(jnp.float32) * root_scale + 2.0 * placed).astype(
        jnp.bfloat16
    )
    margin_row = lax.all_gather(margin, "col", axis=1, tiled=True)
    pulled = (
        2.0 * jnp.dot(margin_row, solved_all, preferred_element_type=jnp.float32) * weights[None, :]
    ).astype(jnp.bfloat16)
    pulled_all = lax.all_gather(pulled, "row", axis=0, tiled=True)
    grad_links = lax.psum_scatter(
        jnp.dot(pulled_all, factor.T, preferred_element_type=jnp.float32),
        "col",
        scatter_dimension=0,
        tiled=True,
    ).astype(jnp.bfloat16)
    grad_factor = jnp.dot(links_all.T, pulled_all, preferred_element_type=jnp.float32)
    grad_factor = (grad_factor + 2.0 * factor.astype(jnp.float32) * weights[None, :]).astype(
        jnp.bfloat16
    )
    return (grad_root, grad_factor[None], grad_links[None])


def solution(mesh):
    return jax.shard_map(
        local,
        mesh=mesh,
        in_specs=(
            P(("grp", "row"), "col"),
            P("grp", "row", "col"),
            P("grp", "col", "row"),
            P("grp", "col"),
            P("col"),
            P(),
        ),
        out_specs=(P(("grp", "row"), "col"), P("grp", "row", "col"), P("grp", "col", "row")),
        check_vma=False,
    )
```

profile of v0, /device:TPU:1, one launch (start us, length us, event | category | flops | bytes accessed | tf_op | source)
XLA Modules:
  0.0 578.5 jit_solution(17137444513439801942)
XLA Ops:
  7.2 0.7 all-gather.15.cloned.1.call-update
  7.9 31.4 %all-gather.15.cloned.1.call-done = bf16[1,1536,512]{2,1,0:T(8,128)(2,1)} async-done(((bf16[1,384,512]{2,1,0:T(8,128)(2,1)}), bf16[1,1536,512]{2,1,0:T(8,128)(2,1)}) %all-gather.15.cloned.1.call-update) | async-done | bytes 1572880 | tf_op jit(solution)/shard_map/all_gather | solution.py:44
  39.4 10.0 %fusion.6 = f32[1536,2048]{1,0:T(8,128)} fusion(bf16[1,512,2048]{2,1,0:T(8,128)(2,1)} %param.7, bf16[1,1536,512]{2,1,0:T(8,128)(2,1)} %all-gather.15.cloned.1.call-done), kind=kOutput, calls=%fused_computation.12 | convolution fusion | flops 3221225472 | bytes 16252928 | tf_op jit(solution)/shard_map/dot_general | solution.py:46
  49.4 0.0 all-gather.7.cloned.1.call-start
  49.5 94.5 %reduce-scatter.5.cloned.1.call-done = f32[96,2048]{1,0:T(8,128)} async-done(((f32[1536,2048]{1,0:T(8,128)}), f32[96,2048]{1,0:T(8,128)}) %reduce-scatter.5.cloned.1.call-update) | async-done | bytes 786448 | tf_op jit(solution)/shard_map/reduce_scatter | solution.py:45
  144.0 1.9 convert_element_type.47
  146.0 2.2 copy.20
  148.3 0.6 copy-done.9
  148.8 1.8 fusion.13
  150.6 2.1 copy.11
  152.8 1.8 fusion.14
  154.6 2.2 copy.12
  156.7 1.7 pad_maximum_fusion.1
  158.5 0.6 copy-done.7
  159.1 48.1 %all-gather.7.cloned.1.call-done = bf16[1536,2048]{1,0:T(8,128)(2,1)} async-done(((bf16[96,2048]{1,0:T(8,128)(2,1)}), bf16[1536,2048]{1,0:T(8,128)(2,1)}) %all-gather.7.cloned.1.call-update) | async-done | bytes 6291472 | tf_op jit(solution)/shard_map/all_gather | solution.py:51
  207.2 5.7 fusion.19
  213.0 60.0 %all-reduce.2.cloned.1.call-done = bf16[384,2,1536]{0,2,1:T(8,128)(2,1)} async-done(((bf16[384,2,1536]{0,2,1:T(8,128)(2,1)}), bf16[384,2,1536]{0,2,1:T(8,128)(2,1)}) %all-reduce.2.cloned.1.call-update) | async-done | bytes 2359312 | tf_op jit(solution)/shard_map/psum | solution.py:29
  273.0 2.4 fusion.17
  275.4 0.9 fusion.18
  276.3 2.5 pad_maximum_fusion
  278.9 16.9 %reduce-scatter.7.cloned.1.call-done = f32[384,96]{0,1:T(8,128)} async-done(((f32[1536,96]{0,1:T(8,128)}), f32[384,96]{0,1:T(8,128)}) %reduce-scatter.7.cloned.1.call-update) | async-done | bytes 147472 | tf_op jit(solution)/shard_map/reduce_scatter | solution.py:53
  295.8 1.6 convert_element_type.50
  297.5 85.5 %reduce-scatter.9.cloned.1.call-done = f32[96,384]{1,0:T(8,128)} async-done(((f32[3072,384]{1,0:T(8,128)}), f32[96,384]{1,0:T(8,128)}) %reduce-scatter.9.cloned.1.call-update) | async-done | bytes 147472 | tf_op jit(solution)/shard_map/reduce_scatter | solution.py:38
  383.0 0.9 convert_element_type.52
  383.9 10.0 %all_gather.22 = bf16[96,1536]{1,0:T(8,128)(2,1)S(1)} all-gather(bf16[96,384]{1,0:T(8,128)(2,1)S(1)} %convert_element_type.52), channel_id=1, replica_groups=mesh['grp'=2,'row'=16,'col'=4] {'col'}, dimensions={1}, use_global_device_ids=true | all-gather | bytes 368640 | tf_op jit(solution)/shard_map/all_gather | solution.py:85
  394.0 4.7 fusion.3
  398.7 0.2 all-gather.11.cloned.1.call-start
  399.0 32.1 %all-gather.9.cloned.1.call-done = bf16[384,3072]{0,1:T(8,128)(2,1)} async-done(((bf16[384,96]{0,1:T(8,128)(2,1)}), bf16[384,3072]{0,1:T(8,128)(2,1)}) %all-gather.9.cloned.1.call-update) | async-done | bytes 2359312 | tf_op jit(solution)/shard_map/all_gather | solution.py:59
  431.0 2.2 fusion.15
  433.3 0.8 fusion.16
  434.1 0.9 pad_maximum_fusion.2
  435.0 58.7 %all-gather.13.cloned.1.call-done = bf16[1536,2048]{1,0:T(8,128)(2,1)} async-done(((bf16[96,2048]{1,0:T(8,128)(2,1)}), bf16[1536,2048]{1,0:T(8,128)(2,1)}) %all-gather.13.cloned.1.call-update) | async-done | bytes 6291472 | tf_op jit(solution)/shard_map/all_gather | solution.py:89
  493.8 8.6 %fusion.4 = f32[1536,512]{1,0:T(8,128)} fusion(bf16[1536,2048]{1,0:T(8,128)(2,1)} %all-gather.13.cloned.1.call-done, bf16[1,512,2048]{2,1,0:T(8,128)(2,1)} %param.7), kind=kOutput, calls=%fused_computation.10 | convolution fusion | flops 3221225472 | bytes 11534336 | tf_op jit(solution)/shard_map/dot_general | solution.py:91
  502.4 1.6 copy-done.3
  504.0 2.5 copy.13
  506.5 22.5 %all-gather.11.cloned.1.call-done = bf16[384,2,1536]{2,0,1:T(8,128)(2,1)} async-done(((bf16[384,2,384]{2,0,1:T(8,128)(2,1)}), bf16[384,2,1536]{2,0,1:T(8,128)(2,1)}) %all-gather.11.cloned.1.call-update) | async-done | bytes 2359312 | tf_op jit(solution)/shard_map/all_gather | solution.py:73
  528.9 3.0 copy.14
  532.0 1.3 fusion.33
  533.3 1.4 copy.18
  534.7 2.3 copy.19
  537.0 0.9 fusion.9
  537.9 0.9 add_multiply_fusion
  538.9 1.1 copy-done
  540.0 2.9 fusion
  542.9 3.7 fusion.2
  546.6 2.4 copy.17
  549.0 20.8 %reduce-scatter.11.cloned.1.call-done = f32[384,512]{1,0:T(8,128)} async-done(((f32[1536,512]{1,0:T(8,128)}), f32[384,512]{1,0:T(8,128)}) %reduce-scatter.11.cloned.1.call-update) | async-done | bytes 786448 | tf_op jit(solution)/shard_map/reduce_scatter | solution.py:90
  569.7 1.9 convert_bitcast_fusion
  (51 shorter events, 0.6 us)
Async XLA Ops:
  7.2 32.2 %all-gather.15.cloned.1.call-start = ((), (), s32[]{:S(2)}) async-start(), calls=%async_computation.13 | async-start | bytes 1966080 | tf_op jit(solution)/shard_map/all_gather | solution.py:44
  7.9 136.1 %reduce-scatter.5.cloned.1.call-start = ((), (), s32[]{:S(2)}) async-start(), calls=%async_computation.5 | async-start | bytes 13369344 | tf_op jit(solution)/shard_map/reduce_scatter | solution.py:45
  49.4 157.8 %all-gather.7.cloned.1.call-start = ((), (), s32[]{:S(2)}) async-start(), calls=%async_computation.6 | async-start | bytes 6684672 | tf_op jit(solution)/shard_map/all_gather | solution.py:51
  145.9 127.1 %all-reduce.2.cloned.1.call-start = ((), (), s32[]{:S(2)}) async-start(), calls=%async_computation.4 | async-start | bytes 4718592 | tf_op jit(solution)/shard_map/psum | solution.py:29
  146.0 2.3 copy-start.11
  148.3 0.6 copy-start.9
  158.4 0.7 copy-start.7
  158.4 48.8 %copy-start.1 = (bf16[96,2048]{1,0:T(8,128)(2,1)S(1)}, bf16[96,2048]{1,0:T(8,128)(2,1)}, u32[]{:S(2)}) copy-start(bf16[96,2048]{1,0:T(8,128)(2,1)} %convert_element_type.47) | copy-start | bytes 1179652
  158.4 137.4 %reduce-scatter.7.cloned.1.call-start = ((), (), s32[]{:S(2)}) async-start(), calls=%async_computation.7 | async-start | bytes 737280 | tf_op jit(solution)/shard_map/reduce_scatter | solution.py:53
  212.9 170.1 %reduce-scatter.9.cloned.1.call-start = ((), (), s32[]{:S(2)}) async-start(), calls=%async_computation.10 | async-start | bytes 4866048 | tf_op jit(solution)/shard_map/reduce_scatter | solution.py:38
  273.0 2.4 copy-start.2
  278.8 152.2 %all-gather.9.cloned.1.call-start = ((), (), s32[]{:S(2)}) async-start(), calls=%async_computation.8 | async-start | bytes 2433024 | tf_op jit(solution)/shard_map/all_gather | solution.py:59
  297.4 196.4 %all-gather.13.cloned.1.call-start = ((), (), s32[]{:S(2)}) async-start(), calls=%async_computation.11 | async-start | bytes 6684672 | tf_op jit(solution)/shard_map/all_gather | solution.py:89
  297.5 101.2 %copy-start.5 = (f32[2048]{0:T(1024)}, f32[2048]{0:T(1024)S(1)}, u32[]{:S(2)}) copy-start(f32[2048]{0:T(1024)S(1)} %broadcast_multiply_fusion) | copy-start | bytes 24580
  398.7 130.2 %all-gather.11.cloned.1.call-start = ((), (), s32[]{:S(2)}) async-start(), calls=%async_computation.9 | async-start | bytes 2949120 | tf_op jit(solution)/shard_map/all_gather | solution.py:73
  431.0 2.2 copy-start.12
  435.0 134.8 %reduce-scatter.11.cloned.1.call-start = ((), (), s32[]{:S(2)}) async-start(), calls=%async_computation.12 | async-start | bytes 3932160 | tf_op jit(solution)/shard_map/reduce_scatter | solution.py:90
  502.4 1.6 copy-start.3
  504.0 2.5 copy-start.8
  534.7 2.3 copy-start.10
  537.0 5.8 %slice-start = ((s8[6291456]{0:T(1024)(128)(4,1)}), s8[4194304]{0:T(1024)(128)(4,1)S(1)}, s32[]{:S(2)}) async-start(s8[6291456]{0:T(1024)(128)(4,1)} %bitcast.102), calls=%async_computation.14 | async-start | bytes 8388608
  537.9 2.0 copy-start
  537.9 4.9 slice-start.1
  539.9 2.9 copy-start.4
  539.9 2.9 copy-start.6
  540.0 2.9 copy-start.13
Sparse Core Ops, SparseCore 0:
  9.6 29.7 all-gather.14
  49.5 94.3 reduce-scatter.4
  146.7 60.5 all-gather.6
  210.0 62.8 all-reduce.1
  275.8 19.9 reduce-scatter.6
  299.4 83.5 reduce-scatter.8
  385.8 45.1 all-gather.8
  433.7 59.9 all-gather.12
  496.0 32.8 all-gather.10
  531.2 38.4 reduce-scatter.10
where the time goes:
time: 579 us
  waiting for transfers between devices  471 us (81%)
  matrix products  44.4 us (8%)
  local copies, waits for them, and re-layouts  23.3 us (4%)
  between operations  14.4 us (2%)
  other arithmetic  14.3 us (2%)
  blocking collectives  10 us (2%)
    reduce_scatter x1, waiting for transfers between devices, local(): lax.psum_scatter(jnp.dot(links_all, factor, preferred_element_type=jnp.fl...  94.5 us
    reduce_scatter x1, waiting for transfers between devices, local(): lax.psum_scatter(margin_part, ('grp', 'row'), scatter_dimension=0, tiled=...  85.5 us
    psum x1, waiting for transfers between devices, local(): selected = lax.psum(picked.astype(jnp.bfloat16), 'col')  60 us
    all_gather x1, waiting for transfers between devices, local(): pulled_all = lax.all_gather(pulled, 'row', axis=0, tiled=True)  58.7 us
    all_gather x1, waiting for transfers between devices, local(): solved_all = lax.all_gather(solved, 'row', axis=0, tiled=True)  48.1 us
    all_gather x1, waiting for transfers between devices, local(): lax.all_gather(adjoint_t, ('grp', 'row'), axis=1, tiled=True)  32.1 us
    all_gather x1, waiting for transfers between devices, local(): links_all = lax.all_gather(links, 'col', axis=0, tiled=True)  31.4 us
    all_gather x1, waiting for transfers between devices, local(): lax.all_gather(lifted, 'col', axis=2, tiled=True)  22.5 us
  transfers between devices with their start and end apart: 10, of which 10 were waited for; matrix products, arithmetic and copies ran while one was open for 11% of the time, Pallas kernels for 0%

commit v1 on v0

--- a/solution.py
+++ b/solution.py
@@ -4,6 +4,28 @@
 from jax.sharding import PartitionSpec as P
 
 BW = 128
+
+
+def joined_along(blocks, dim):
+    blocks = jnp.moveaxis(blocks, 0, dim)
+    dims = blocks.shape
+    return blocks.reshape(*dims[:dim], dims[dim] * dims[dim + 1], *dims[dim + 2 :])
+
+
+def gather_around(x, axis, dim):
+    length = lax.axis_size(axis)
+    pairs = [(i, (i + 1) % length) for i in range(length)]
+    back = [(b, a) for a, b in pairs]
+    lower, upper = ([], [])
+    for hop in range(length - 1):
+        if hop % 2 == 0:
+            lower.append(lax.ppermute(lower[-1] if lower else x, axis, pairs))
+        else:
+            upper.append(lax.ppermute(upper[-1] if upper else x, axis, back))
+    tiles = jnp.stack([*lower[::-1], x, *upper])
+    shift = lax.axis_index(axis) - len(lower)
+    tiles = tiles[(jnp.arange(length) - shift) % length]
+    return joined_along(tiles, dim)
 
 
 def local(root_inverse, child_inverse, coupling, child_weights, root_weights, parent_blocks):
@@ -41,7 +63,7 @@
     factor = child_inverse[0]
     links = coupling[0]
     weights = child_weights[0].astype(jnp.float32)
-    links_all = lax.all_gather(links, "col", axis=0, tiled=True)
+    links_all = gather_around(links, "col", 0)
     solved = lax.psum_scatter(
         jnp.dot(links_all, factor, preferred_element_type=jnp.float32),
         "row",

time: 579 us -> 521 us (0.90)
  waiting for transfers between devices: 471 us -> 410 us
    psum x1, waiting for transfers between devices: 60 us -> 7.29 us  [local(): selected = lax.psum(picked.astype(jnp.bfloat16), 'col')]
    all_gather x1 -> x0, waiting for transfers between devices: 31.4 us -> none  [local(): links_all = lax.all_gather(links, 'col', axis=0, tiled=True)]
    ppermute x0 -> x3, waiting for transfers between devices: none -> 19.5 us  [the longest x2 19.5 us: gather_around(): lower.append(lax.ppermute(lower[-1] if lower else x, axis, pairs))]
    unnamed x37 -> x27, local copies, waits for them, and re-layouts: 14.7 us -> 9.86 us
  transfers between devices with their start and end apart: 10 -> 12, of which waited for: 10 -> 11; matrix products, arithmetic and copies ran while one was open for 11% -> 12% of each run, Pallas kernels for 0% -> 0%
where the time goes in v1:
time: 521 us; the launch traced here: 520 us
  waiting for transfers between devices  410 us (79%)
  matrix products  43.8 us (8%)
  local copies, waits for them, and re-layouts  19.5 us (4%)
  between operations  15.8 us (3%)
  other arithmetic  15.6 us (3%)
  blocking collectives  10 us (2%)
  starting transfers between devices  5.3 us (1%)
    reduce_scatter x1, waiting for transfers between devices, local(): lax.psum_scatter(jnp.dot(links_all, factor, preferred_element_type=jnp.fl...  94.8 us
    reduce_scatter x1, waiting for transfers between devices, local(): lax.psum_scatter(margin_part, ('grp', 'row'), scatter_dimension=0, tiled=...  86.3 us
    all_gather x1, waiting for transfers between devices, local(): pulled_all = lax.all_gather(pulled, 'row', axis=0, tiled=True)  58.6 us
    all_gather x1, waiting for transfers between devices, local(): solved_all = lax.all_gather(solved, 'row', axis=0, tiled=True)  48.7 us
    all_gather x1, waiting for transfers between devices, local(): lax.all_gather(adjoint_t, ('grp', 'row'), axis=1, tiled=True)  32.1 us
    all_gather x1, waiting for transfers between devices, local(): lax.all_gather(lifted, 'col', axis=2, tiled=True)  25.8 us
    reduce_scatter x1, waiting for transfers between devices, local(): lax.psum_scatter(jnp.dot(pulled_all, factor.T, preferred_element_type=jnp...  20.4 us
    ppermute x2, waiting for transfers between devices, gather_around(): lower.append(lax.ppermute(lower[-1] if lower else x, axis, pairs))  19.5 us
  transfers between devices with their start and end apart: 12, of which 11 were waited for; matrix products, arithmetic and copies ran while one was open for 12% of the time, Pallas kernels for 0%

profile of v1, /device:TPU:1, one launch (start us, length us, event | category | flops | bytes accessed | tf_op | source)
XLA Modules:
  0.0 519.9 jit_solution(13768307647754515620)
XLA Ops:
  8.0 2.5 collective-permute-start
  10.6 2.2 collective-permute-start.2
  12.8 8.9 %collective-permute-done = bf16[384,512]{1,0:T(8,128)(2,1)S(1)} collective-permute-done((bf16[384,512]{1,0:T(8,128)(2,1)}, bf16[384,512]{1,0:T(8,128)(2,1)S(1)}, u32[]{:S(2)}, u32[]{:S(2)}) %collective-permute-start) | collective-permute-done | bytes 393248 | tf_op jit(solution)/shard_map/ppermute | solution.py:22
  21.8 10.6 %collective-permute-done.1 = bf16[384,512]{1,0:T(8,128)(2,1)S(1)} collective-permute-done((bf16[384,512]{1,0:T(8,128)(2,1)S(1)}, bf16[384,512]{1,0:T(8,128)(2,1)S(1)}, u32[]{:S(2)}, u32[]{:S(2)}) %collective-permute-start.1) | collective-permute-done | bytes 393248 | tf_op jit(solution)/shard_map/ppermute | solution.py:22
  32.4 1.2 pad_maximum_fusion.2
  33.5 0.6 gather_fusion
  34.2 8.5 %fusion.5 = f32[1536,2048]{1,0:T(8,128)} fusion(bf16[1536,512]{1,0:T(8,128)(2,1)S(1)} %bitcast.96, bf16[1,512,2048]{2,1,0:T(8,128)(2,1)} %param.7), kind=kOutput, calls=%fused_computation.12 | convolution fusion | flops 3221225472 | bytes 16252928 | tf_op jit(solution)/shard_map/dot_general | solution.py:68
  42.8 94.8 %reduce-scatter.5.cloned.1.call-done = f32[96,2048]{1,0:T(8,128)} async-done(((f32[1536,2048]{1,0:T(8,128)}), f32[96,2048]{1,0:T(8,128)}) %reduce-scatter.5.cloned.1.call-update) | async-done | bytes 786448 | tf_op jit(solution)/shard_map/reduce_scatter | solution.py:67
  137.5 1.9 convert_element_type.47
  139.6 2.2 copy.16
  141.8 1.8 fusion.10
  143.6 2.1 copy.9
  145.8 1.8 fusion.11
  147.6 2.1 copy.10
  149.7 1.7 pad_maximum_fusion.1
  151.5 0.6 copy-done.5
  152.1 48.7 %all-gather.5.cloned.1.call-done = bf16[1536,2048]{1,0:T(8,128)(2,1)} async-done(((bf16[96,2048]{1,0:T(8,128)(2,1)}), bf16[1536,2048]{1,0:T(8,128)(2,1)}) %all-gather.5.cloned.1.call-update) | async-done | bytes 6291472 | tf_op jit(solution)/shard_map/all_gather | solution.py:73
  200.8 5.7 %fusion.16 = f32[1536,96]{0,1:T(8,128)} fusion(bf16[1536,2048]{1,0:T(8,128)(2,1)} %all-gather.5.cloned.1.call-done, bf16[96,2048]{1,0:T(8,128)(2,1)S(1)} %copy-done.1, f32[2048]{0:T(1024)S(1)} %bitcast.103), kind=kOutput, calls=%fused_computation.34 | convolution fusion | flops 604569600 | bytes 7282688 | tf_op jit(solution)/shard_map/dot_general | solution.py:76
  206.5 7.3 %all-reduce.2.cloned.1.call-done = bf16[384,2,1536]{0,2,1:T(8,128)(2,1)} async-done(((bf16[384,2,1536]{0,2,1:T(8,128)(2,1)}), bf16[384,2,1536]{0,2,1:T(8,128)(2,1)}) %all-reduce.2.cloned.1.call-update) | async-done | bytes 2359312 | tf_op jit(solution)/shard_map/psum | solution.py:51
  213.8 2.4 fusion.14
  216.2 0.9 fusion.15
  217.1 2.5 pad_maximum_fusion
  219.7 16.4 %reduce-scatter.7.cloned.1.call-done = f32[384,96]{0,1:T(8,128)} async-done(((f32[1536,96]{0,1:T(8,128)}), f32[384,96]{0,1:T(8,128)}) %reduce-scatter.7.cloned.1.call-update) | async-done | bytes 147472 | tf_op jit(solution)/shard_map/reduce_scatter | solution.py:75
  236.2 1.6 convert_element_type.50
  237.8 86.3 %reduce-scatter.9.cloned.1.call-done = f32[96,384]{1,0:T(8,128)} async-done(((f32[3072,384]{1,0:T(8,128)}), f32[96,384]{1,0:T(8,128)}) %reduce-scatter.9.cloned.1.call-update) | async-done | bytes 147472 | tf_op jit(solution)/shard_map/reduce_scatter | solution.py:60
  324.1 0.9 convert_element_type.52
  325.0 10.0 %all_gather.18 = bf16[96,1536]{1,0:T(8,128)(2,1)S(1)} all-gather(bf16[96,384]{1,0:T(8,128)(2,1)S(1)} %convert_element_type.52), channel_id=1, replica_groups=mesh['grp'=2,'row'=16,'col'=4] {'col'}, dimensions={1}, use_global_device_ids=true | all-gather | bytes 368640 | tf_op jit(solution)/shard_map/all_gather | solution.py:107
  335.0 4.7 fusion.2
  339.8 0.2 all-gather.9.cloned.1.call-start
  340.0 32.1 %all-gather.7.cloned.1.call-done = bf16[384,3072]{0,1:T(8,128)(2,1)} async-done(((bf16[384,96]{0,1:T(8,128)(2,1)}), bf16[384,3072]{0,1:T(8,128)(2,1)}) %all-gather.7.cloned.1.call-update) | async-done | bytes 2359312 | tf_op jit(solution)/shard_map/all_gather | solution.py:81
  372.1 2.2 fusion.13
  374.3 0.8 fusion.12
  375.1 0.9 pad_maximum_fusion.3
  376.1 58.6 %all-gather.11.cloned.1.call-done = bf16[1536,2048]{1,0:T(8,128)(2,1)} async-done(((bf16[96,2048]{1,0:T(8,128)(2,1)}), bf16[1536,2048]{1,0:T(8,128)(2,1)}) %all-gather.11.cloned.1.call-update) | async-done | bytes 6291472 | tf_op jit(solution)/shard_map/all_gather | solution.py:111
  434.7 8.6 %fusion.3 = f32[1536,512]{1,0:T(8,128)} fusion(bf16[1536,2048]{1,0:T(8,128)(2,1)} %all-gather.11.cloned.1.call-done, bf16[1,512,2048]{2,1,0:T(8,128)(2,1)} %param.7), kind=kOutput, calls=%fused_computation.10 | convolution fusion | flops 3221225472 | bytes 11534336 | tf_op jit(solution)/shard_map/dot_general | solution.py:113
  443.3 0.7 copy-done.6
  443.9 25.8 %all-gather.9.cloned.1.call-done = bf16[384,2,1536]{2,0,1:T(8,128)(2,1)} async-done(((bf16[384,2,384]{2,0,1:T(8,128)(2,1)}), bf16[384,2,1536]{2,0,1:T(8,128)(2,1)}) %all-gather.9.cloned.1.call-update) | async-done | bytes 2359312 | tf_op jit(solution)/shard_map/all_gather | solution.py:95
  469.7 3.0 copy.11
  472.7 1.7 fusion.32
  474.4 2.3 copy.15
  476.7 2.3 copy.14
  479.1 0.9 fusion.8
  480.0 0.9 add_multiply_fusion
  480.9 1.7 copy-done
  482.6 2.9 fusion
  485.5 4.6 fusion.1
  490.1 20.4 %reduce-scatter.11.cloned.1.call-done = f32[384,512]{1,0:T(8,128)} async-done(((f32[1536,512]{1,0:T(8,128)}), f32[384,512]{1,0:T(8,128)}) %reduce-scatter.11.cloned.1.call-update) | async-done | bytes 786448 | tf_op jit(solution)/shard_map/reduce_scatter | solution.py:112
  510.5 1.9 convert_bitcast_fusion
  (48 shorter events, 0.6 us)
Async XLA Ops:
  8.0 129.5 %reduce-scatter.5.cloned.1.call-start = ((), (), s32[]{:S(2)}) async-start(), calls=%async_computation.5 | async-start | bytes 13369344 | tf_op jit(solution)/shard_map/reduce_scatter | solution.py:67
  8.0 13.7 %collective-permute-start = (bf16[384,512]{1,0:T(8,128)(2,1)}, bf16[384,512]{1,0:T(8,128)(2,1)S(1)}, u32[]{:S(2)}, u32[]{:S(2)}) collective-permute-start(bf16[384,512]{1,0:T(8,128)(2,1)} %bitcast.98), channel_id=1, source_target_pairs={{0,1},{1,2},{2,3},{3,0},{4,5},{5,6},{6,7},{7,4},{8,9},{9,10},{10,1... | collective-permute-start | bytes 1179656 | tf_op jit(solution)/shard_map/ppermute | solution.py:22
  10.6 11.2 %collective-permute-start.2 = (bf16[384,512]{1,0:T(8,128)(2,1)}, bf16[384,512]{1,0:T(8,128)(2,1)S(1)}, u32[]{:S(2)}, u32[]{:S(2)}) collective-permute-start(bf16[384,512]{1,0:T(8,128)(2,1)} %bitcast.99), channel_id=1, source_target_pairs={{1,0},{2,1},{3,2},{0,3},{5,4},{6,5},{7,6},{4,7},{9,8},{10,9},{11,1... | collective-permute-start | bytes 1179656 | tf_op jit(solution)/shard_map/ppermute | solution.py:24
  21.7 10.6 %collective-permute-start.1 = (bf16[384,512]{1,0:T(8,128)(2,1)S(1)}, bf16[384,512]{1,0:T(8,128)(2,1)S(1)}, u32[]{:S(2)}, u32[]{:S(2)}) collective-permute-start(bf16[384,512]{1,0:T(8,128)(2,1)S(1)} %collective-permute-done), channel_id=1, source_target_pairs={{0,1},{1,2},{2,3},{3,0},{4,5},{5,6},{6,7},{7,4},{8,9},{9,10},{10,1... | collective-permute-start | bytes 1179656 | tf_op jit(solution)/shard_map/ppermute | solution.py:22
  34.2 8.5 %copy-start.3 = (bf16[4,384,512]{2,1,0:T(8,128)(2,1)}, bf16[4,384,512]{2,1,0:T(8,128)(2,1)S(1)}, u32[]{:S(2)}) copy-start(bf16[4,384,512]{2,1,0:T(8,128)(2,1)S(1)} %gather_fusion) | copy-start | bytes 4718596
  42.7 158.0 %all-gather.5.cloned.1.call-start = ((), (), s32[]{:S(2)}) async-start(), calls=%async_computation.6 | async-start | bytes 6684672 | tf_op jit(solution)/shard_map/all_gather | solution.py:73
  139.5 74.3 %all-reduce.2.cloned.1.call-start = ((), (), s32[]{:S(2)}) async-start(), calls=%async_computation.4 | async-start | bytes 4718592 | tf_op jit(solution)/shard_map/psum | solution.py:51
  139.5 2.3 copy-start.7
  151.4 0.7 copy-start.5
  151.4 49.4 %copy-start.1 = (bf16[96,2048]{1,0:T(8,128)(2,1)S(1)}, bf16[96,2048]{1,0:T(8,128)(2,1)}, u32[]{:S(2)}) copy-start(bf16[96,2048]{1,0:T(8,128)(2,1)} %convert_element_type.47) | copy-start | bytes 1179652
  151.4 84.8 %reduce-scatter.7.cloned.1.call-start = ((), (), s32[]{:S(2)}) async-start(), calls=%async_computation.7 | async-start | bytes 737280 | tf_op jit(solution)/shard_map/reduce_scatter | solution.py:75
  206.5 117.6 %reduce-scatter.9.cloned.1.call-start = ((), (), s32[]{:S(2)}) async-start(), calls=%async_computation.10 | async-start | bytes 4866048 | tf_op jit(solution)/shard_map/reduce_scatter | solution.py:60
  213.8 2.4 copy-start.2
  219.7 152.4 %all-gather.7.cloned.1.call-start = ((), (), s32[]{:S(2)}) async-start(), calls=%async_computation.8 | async-start | bytes 2433024 | tf_op jit(solution)/shard_map/all_gather | solution.py:81
  237.8 196.9 %all-gather.11.cloned.1.call-start = ((), (), s32[]{:S(2)}) async-start(), calls=%async_computation.11 | async-start | bytes 6684672 | tf_op jit(solution)/shard_map/all_gather | solution.py:111
  339.8 129.9 %all-gather.9.cloned.1.call-start = ((), (), s32[]{:S(2)}) async-start(), calls=%async_computation.9 | async-start | bytes 2949120 | tf_op jit(solution)/shard_map/all_gather | solution.py:95
  372.1 2.2 copy-start.8
  376.0 134.5 %reduce-scatter.11.cloned.1.call-start = ((), (), s32[]{:S(2)}) async-start(), calls=%async_computation.12 | async-start | bytes 3932160 | tf_op jit(solution)/shard_map/reduce_scatter | solution.py:112
  443.3 0.7 copy-start.6
  479.1 6.4 %slice-start = ((s8[6291456]{0:T(1024)(128)(4,1)}), s8[4194304]{0:T(1024)(128)(4,1)S(1)}, s32[]{:S(2)}) async-start(s8[6291456]{0:T(1024)(128)(4,1)} %bitcast.105), calls=%async_computation.13 | async-start | bytes 8388608
  480.0 2.6 copy-start
  480.0 5.5 %slice-start.1 = ((s8[6291456]{0:T(1024)(128)(4,1)}), s8[2097152]{0:T(1024)(128)(4,1)S(1)}, s32[]{:S(2)}) async-start(s8[6291456]{0:T(1024)(128)(4,1)} %bitcast.105), calls=%async_computation.14 | async-start | bytes 4194304
  482.6 2.9 copy-start.4
  482.6 2.9 copy-start.9
Sparse Core Ops, SparseCore 0:
  42.8 94.6 reduce-scatter.4
  140.2 60.4 all-gather.4
Sparse Core Ops, SparseCore 1:
  151.5 62.3 all-reduce.1
  216.7 19.4 reduce-scatter.6
  239.8 84.3 reduce-scatter.8
  326.9 45.1 all-gather.6
  374.8 59.8 all-gather.10
  436.9 32.7 all-gather.8
  472.0 38.5 reduce-scatter.10
